TPU v7x, 256 devices: a whole 4x4x8 slice. The times are simulated.
256 devices in a mesh: row: 16 (over z_lo, y), col: 16 (over z_hi, x, core).
Axes of the slice: x: 4, y: 4, z: 8 (z_hi: 2, z_lo: 4; z = z_hi * 4 + z_lo), core: 2. Of those that a mesh axis runs over, the one named last changes fastest.
Arguments:
- gradient: bfloat16 [512, 28672], P('col', 'row'), may hold values from -6 to 6
- basis: bfloat16 [28672, 28672], P('row', 'col'), may hold values from -0.03125 to 0.03125
- eigen: float32 [512, 28672], P('row', 'col'), may hold values from 0.2 to 5
Outputs:
- result: bfloat16 [512, 28672], P('col', 'row')
All inputs are finite; a program needn't handle non-finite values.
Results may differ from a plain program's by a relative error of at most 0.0044.
Values may be sent and summed in bfloat16 or wider, within the bound.
A program may use at most 64 MiB of HBM per device.

v0:
```python
import jax
import jax.numpy as jnp
from jax import lax
from jax.sharding import Mesh
from jax.sharding import PartitionSpec as P

COL = ("col_0", "col_1", "col_2")


def sent_to_all(shard, axis):
    count = lax.axis_size(axis)
    return lax.all_to_all(
        jnp.broadcast_to(shard[None], (count, *shard.shape)), axis, 0, 0, tiled=True
    )


def laid_out(tiles, dim):
    dims = list(tiles.shape[1:])
    dims[dim] *= tiles.shape[0]
    return jnp.moveaxis(tiles, 0, dim).reshape(dims)


def gather_axes(shard, axes, dim):
    far, near = axes
    tiles = sent_to_all(sent_to_all(shard, far), near)
    return laid_out(tiles.swapaxes(0, 1).reshape(-1, *shard.shape), dim)


def gathered_copies(shard, axis, dim):
    tiles = sent_to_all(shard, axis)
    return laid_out(tiles, dim)


def split_up(shard, dim, count):
    dims = shard.shape
    tiles = shard.reshape(*dims[:dim], count, dims[dim] // count, *dims[dim + 1 :])
    return jnp.moveaxis(tiles, dim, 0)


def sum_at_owner(shard, axis, dim):
    tiles = split_up(shard, dim, lax.axis_size(axis))
    arrived = lax.all_to_all(tiles, axis, split_axis=0, concat_axis=0, tiled=True)
    return arrived.sum(axis=0)


def sum_by_axis(shard, axes, dim):
    far, near = axes
    own = sum_at_owner(split_up(shard, dim, lax.axis_size(far)), near, dim + 1)
    return jnp.sum(lax.all_to_all(own, far, 0, 0, tiled=True), axis=0)


def per_device(gradient, basis, eigen):
    whole_grad = gather_axes(gradient, (("col_0", "col_1"), "col_2"), 0)
    part = whole_grad
    rotated = lax.psum_scatter(
        jnp.dot(part, basis, preferred_element_type=jnp.float32),
        "row",
        scatter_dimension=0,
        tiled=True,
    )
    scaled = (rotated / eigen).astype(jnp.bfloat16)
    full_scaled = gathered_copies(scaled, "row", 0)
    part = full_scaled
    result = sum_by_axis(
        lax.dot_general(part, basis, (((1,), (1,)), ((), ())), preferred_element_type=jnp.float32),
        (("col_0", "col_1"), "col_2"),
        0,
    )
    return result.astype(jnp.bfloat16)


def solution(mesh):
    finer = Mesh(
        mesh.devices.reshape(mesh.shape["row"], 2, 4, 2), ("row", "col_0", "col_1", "col_2")
    )
    return jax.shard_map(
        per_device,
        mesh=finer,
        in_specs=(P(COL, "row"), P("row", COL), P("row", COL)),
        out_specs=P(COL, "row"),
        check_vma=False,
    )
```

profile of v0, /device:TPU:32, one launch (start us, length us, event | category | flops | bytes accessed | tf_op | source)
XLA Modules:
  0.0 264.3 jit_solution(9207218903607643552)
XLA Ops:
  6.5 0.0 reduce-scatter.2.cloned.1.call-start
  6.5 1.0 broadcast_in_dim.6
  7.5 37.9 %all_to_all.25 = bf16[8,32,1792]{2,1,0:T(8,128)(2,1)S(1)} all-to-all(bf16[8,32,1792]{2,1,0:T(8,128)(2,1)S(1)} %broadcast_in_dim.6), channel_id=1, replica_groups=mesh['row'=16,'col_0'=2,'col_1'=4,'col_2'=2] {'col_0','col_1'}, dimensions={0} | all-to-all | bytes 1835008 | tf_op jit(solution)/shard_map/all_to_all | solution.py:12
  45.4 0.2 broadcast_in_dim.7
  45.6 0.0 copy-start.1
  45.6 5.6 %all_to_all.26 = bf16[2,8,32,1792]{3,2,1,0:T(8,128)(2,1)S(1)} all-to-all(bf16[2,8,32,1792]{3,2,1,0:T(8,128)(2,1)S(1)} %broadcast_in_dim.7), channel_id=1, replica_groups=mesh['row'=16,'col_0'=2,'col_1'=4,'col_2'=2] {'col_2'}, dimensions={0} | all-to-all | bytes 3670016 | tf_op jit(solution)/shard_map/all_to_all | solution.py:12
  51.2 0.1 copy.6
  51.3 0.0 copy-done.1
  51.3 5.3 %fusion.5 = f32[512,1792]{1,0:T(8,128)} fusion(bf16[512,1792]{1,0:T(8,128)(2,1)S(1)} %bitcast.16, bf16[1792,1792]{1,0:T(8,128)(2,1)S(1)} %copy-done.1), kind=kOutput, calls=%fused_computation.4 | convolution fusion | flops 3288334336 | bytes 11927552 | tf_op jit(solution)/shard_map/dot_general | solution.py:56
  56.6 0.0 copy-start
  56.6 0.0 reduce-scatter.2.cloned.1.call-update
  56.6 81.4 %reduce-scatter.2.cloned.1.call-done = f32[32,1792]{1,0:T(8,128)} async-done(((f32[512,1792]{1,0:T(8,128)}), f32[32,1792]{1,0:T(8,128)}) %reduce-scatter.2.cloned.1.call-update) | async-done | bytes 229392 | tf_op jit(solution)/shard_map/reduce_scatter | solution.py:55
  138.0 0.0 copy-done
  138.0 1.0 divide_convert_fusion
  139.0 0.2 broadcast_in_dim.8
  139.2 43.4 %all_to_all.27 = bf16[16,32,1792]{2,1,0:T(8,128)(2,1)S(1)} all-to-all(bf16[16,32,1792]{2,1,0:T(8,128)(2,1)S(1)} %broadcast_in_dim.8), channel_id=1, replica_groups=mesh['row'=16,'col_0'=2,'col_1'=4,'col_2'=2] {'row'}, dimensions={0} | all-to-all | bytes 3670016 | tf_op jit(solution)/shard_map/all_to_all | solution.py:12
  182.6 6.3 %fusion.2 = f32[2,8,32,1792]{3,2,0,1:T(8,128)S(1)} fusion(bf16[8,2,32,1792]{3,2,1,0:T(8,128)(2,1)S(1)} %bitcast.17, bf16[1792,1792]{1,0:T(8,128)(2,1)} %param.4), kind=kOutput, calls=%fused_computation.2 | convolution fusion | flops 3288334336 | bytes 11927552 | tf_op jit(solution)/shard_map/dot_general | solution.py:65
  189.0 0.3 copy.7
  189.2 7.7 %all_to_all.28 = f32[2,8,32,1792]{3,2,1,0:T(8,128)} all-to-all(f32[2,8,32,1792]{3,2,1,0:T(8,128)S(1)} %copy.7), channel_id=1, replica_groups=mesh['row'=16,'col_0'=2,'col_1'=4,'col_2'=2] {'col_2'}, dimensions={0} | all-to-all | bytes 7340032 | tf_op jit(solution)/shard_map/all_to_all | solution.py:42
  196.9 3.7 %reduce_sum.18 = f32[8,32,1792]{2,1,0:T(8,128)} reduce(f32[2,8,32,1792]{3,2,1,0:T(8,128)} %all_to_all.28, f32[]{:T(128)} %constant.0.clone.1), dimensions={0}, to_apply=%region_1.0 | reduce | flops 458752 | bytes 5505028 | tf_op jit(solution)/shard_map/reduce_sum | solution.py:43
  200.6 56.1 %all_to_all.29 = f32[8,32,1792]{2,1,0:T(8,128)S(1)} all-to-all(f32[8,32,1792]{2,1,0:T(8,128)} %reduce_sum.18), channel_id=1, replica_groups=mesh['row'=16,'col_0'=2,'col_1'=4,'col_2'=2] {'col_0','col_1'}, dimensions={0} | all-to-all | bytes 3670016 | tf_op jit(solution)/shard_map/all_to_all | solution.py:49
  256.7 0.8 reduce_sum.19
Async XLA Ops:
  6.5 131.5 %reduce-scatter.2.cloned.1.call-start = ((), (), s32[]{:S(2)}) async-start(), calls=%async_computation.6 | async-start | bytes 3899392 | tf_op jit(solution)/shard_map/reduce_scatter | solution.py:55
  45.6 5.8 %copy-start.1 = (bf16[1792,1792]{1,0:T(8,128)(2,1)S(1)}, bf16[1792,1792]{1,0:T(8,128)(2,1)}, u32[]{:S(2)}) copy-start(bf16[1792,1792]{1,0:T(8,128)(2,1)} %param.4) | copy-start | bytes 19267588
  56.6 81.4 %copy-start = (f32[32,1792]{1,0:T(8,128)S(1)}, f32[32,1792]{1,0:T(8,128)}, u32[]{:S(2)}) copy-start(f32[32,1792]{1,0:T(8,128)} %param.5) | copy-start | bytes 688132
Sparse Core Ops, SparseCore 0:
  56.8 81.2 reduce-scatter.1
where the time goes:
time: 265 us; the launch traced here: 264 us
  blocking collectives  151 us (57%)
  waiting for transfers between devices  81.4 us (31%)
  between operations  13.5 us (5%)
  matrix products  11.6 us (4%)
  other arithmetic  5.45 us (2%)
    all_to_all x3, blocking collectives, sent_to_all(): lax.all_to_all(jnp.broadcast_to(shard[None], (count, *shard.shape)), axis...  86.9 us
    reduce_scatter x1, waiting for transfers between devices, per_device(): lax.psum_scatter(jnp.dot(part, basis, preferred_element_type=jnp.float32)...  81.4 us
    all_to_all x1, blocking collectives, sum_by_axis(): return jnp.sum(lax.all_to_all(own, far, 0, 0, tiled=True), axis=0)  56.1 us
    all_to_all x1, blocking collectives, sum_at_owner(): lax.all_to_all(tiles, axis, split_axis=0, concat_axis=0, tiled=True)  7.7 us
    dot_general x1, matrix products, per_device(): lax.dot_general(part, basis, (((1,), (1,)), ((), ())), preferred_element_...  6.34 us
  transfers between devices with their start and end apart: 1, of which 1 were waited for; matrix products, arithmetic and copies ran while one was open for 0% of the time, Pallas kernels for 0%

commit v1 on v0

v1 whole, which is shorter than its diff:
```python
import functools

import jax
import jax.numpy as jnp
from jax import lax
from jax.experimental import pallas as pl
from jax.experimental.pallas import tpu as pltpu
from jax.sharding import PartitionSpec as P

MESH = pl.DeviceIdType.MESH
HALVES = 2
TILES = 2
NSEM = 192


def kernel(g_ref, b_ref, e_ref, out_ref, basis, eigen, g_all, part, ysend, yrecv, ysum, zsend, zrecv, s_all,
           back, crecv, xsum, xsend, xrecv, tsend, trecv, tsum, ssem, rsem, lsem):
    f32, bf16 = jnp.float32, jnp.bfloat16
    cols = basis.shape[1]
    hr = g_all.shape[2]
    tw = cols // TILES
    r, c = lax.axis_index("row"), lax.axis_index("col")
    z, y = r // 4, r % 4
    zh, x, k = c // 8, (c // 2) % 4, c % 2

    def row_dev(dz, dy):
        return (((z + dz) % 4) * 4 + (y + dy) % 4, c)

    def col_dev(dzh, dx, dk):
        return (r, ((zh + dzh) % 2) * 8 + ((x + dx) % 4) * 2 + (k + dk) % 2)

    def col_id(dzh, dx, dk):
        return ((zh + dzh) % 2) * 8 + ((x + dx) % 4) * 2 + (k + dk) % 2

    count = [0]
    started = []

    def send(src, dst, device):
        i = count[0]
        count[0] += 1
        copy = pltpu.make_async_remote_copy(
            src_ref=src, dst_ref=dst, send_sem=ssem.at[i], recv_sem=rsem.at[i],
            device_id=device, device_id_type=MESH)
        copy.start()
        started.append(copy)
        return copy

    local = [
        pltpu.make_async_copy(b_ref, basis, lsem.at[0]),
        pltpu.make_async_copy(e_ref, eigen, lsem.at[1]),
    ]
    for h in range(HALVES):
        local.append(pltpu.make_async_copy(g_ref.at[pl.ds(h * hr, hr)], g_all.at[h, c], lsem.at[2 + h]))
    for copy in local:
        copy.start()

    barrier = pltpu.get_barrier_semaphore()
    peers = [row_dev(0, 1), row_dev(0, 3), row_dev(1, 0), row_dev(2, 0), row_dev(3, 0),
             col_dev(1, 0, 0), col_dev(0, 1, 0), col_dev(0, 2, 0), col_dev(0, 3, 0), col_dev(0, 0, 1)]
    for peer in peers:
        pl.semaphore_signal(barrier, inc=1, device_id=peer, device_id_type=MESH)
    pl.semaphore_wait(barrier, len(peers))

    spread = {}

    def spread_own(h):
        own = g_ref.at[pl.ds(h * hr, hr)]
        there = g_all.at[h, c]
        spread[h, "z"] = send(own, there, col_dev(1, 0, 0))
        for dx in (1, 3, 2):
            spread[h, "x", dx] = send(own, there, col_dev(0, dx, 0))
        spread[h, "s"] = [send(own, there, col_dev(0, 0, 1))]

    def to_sibling(h, j):
        spread[h, "s"].append(send(g_all.at[h, j], g_all.at[h, j], col_dev(0, 0, 1)))

    def spread_far(h):
        spread[h, "z"].wait_recv()
        j = col_id(1, 0, 0)
        for dx in (1, 3, 2):
            spread[h, "zx", dx] = send(g_all.at[h, j], g_all.at[h, j], col_dev(0, dx, 0))
        to_sibling(h, j)

    def spread_near(h):
        for far, name in ((0, "x"), (1, "zx")):
            for dx in (1, 3, 2):
                spread[h, name, dx].wait_recv()
                to_sibling(h, col_id(far, 4 - dx, 0))

    def spread_end(h):
        for copy in spread[h, "s"]:
            copy.wait_recv()
        local[2 + h].wait()

    ring = {}

    def product(h, t):
        lhs = g_all[h].reshape(-1, cols)
        p = jnp.dot(lhs, basis[:, pl.ds(t * tw, tw)], preferred_element_type=f32)
        part[h, t] = p.reshape(4, 4, hr, tw)

    def y_first(h, t):
        p = part.at[h, t]
        up, down, across = (y + 1) % 4, (y + 3) % 4, (y + 2) % 4
        sb, rb = ysend.at[h, t], yrecv.at[h, t]
        for i, (zs, d, dy) in enumerate(((0, across, 1), (2, across, 3), (2, up, 1), (0, down, 3))):
            for q in range(2):
                sb[i, q] = p[zs + q, d].astype(bf16)
            ring[h, t, i] = send(sb.at[i], rb.at[i], row_dev(0, dy))

    def y_second(h, t):
        p = part.at[h, t]
        sb, rb = ysend.at[h, t], yrecv.at[h, t]
        for i, (zs, dy) in enumerate(((0, 1), (2, 3))):
            ring[h, t, i].wait_recv()
            d = (y + dy) % 4
            for q in range(2):
                sb[4 + i, q] = (p[zs + q, d] + rb[i, q].astype(f32)).astype(bf16)
            ring[h, t, 4 + i] = send(sb.at[4 + i], rb.at[4 + i], row_dev(0, dy))

    def y_end(h, t):
        p = part.at[h, t]
        rb = yrecv.at[h, t]
        for i in (2, 3, 4, 5):
            ring[h, t, i].wait_recv()
        for q in range(2):
            ysum[h, t, q] = p[q, y] + rb[3, q].astype(f32) + rb[4, q].astype(f32)
            ysum[h, t, 2 + q] = p[2 + q, y] + rb[2, q].astype(f32) + rb[5, q].astype(f32)
        for dz in (1, 2, 3):
            zsend[h, t, dz - 1] = ysum[h, t, (z + dz) % 4].astype(bf16)
            ring[h, t, "z", dz] = send(zsend.at[h, t, dz - 1], zrecv.at[h, t, dz - 1], row_dev(dz, 0))

    def tile_of(h, t, i):
        return s_all.at[h, i, :, pl.ds(t * tw, tw)]

    def y_spread(h, t, dz):
        at = tile_of(h, t, ((z + 4 - dz) % 4) * 4 + y)
        for dy in (1, 3):
            ring[h, t, "sy", dz, dy] = send(at, at, row_dev(0, dy))

    def z_end(h, t):
        total = ysum[h, t, z]
        for dz in (1, 2, 3):
            ring[h, t, "z", dz].wait_recv()
            total = total + zrecv[h, t, dz - 1].astype(f32)
        scaled = total / eigen[pl.ds(h * hr, hr), pl.ds(t * tw, tw)]
        s_all[h, r, :, pl.ds(t * tw, tw)] = scaled.astype(bf16)
        at = tile_of(h, t, r)
        for dz in (1, 2, 3):
            ring[h, t, "sz", dz] = send(at, at, row_dev(dz, 0))
        y_spread(h, t, 0)

    def z_spread(h, t):
        for dz in (1, 3, 2):
            ring[h, t, "sz", dz].wait_recv()
            y_spread(h, t, dz)

    def y_relay(h, t):
        for dz in (0, 1, 3, 2):
            dy = 1 if dz < 2 else 3
            ring[h, t, "sy", dz, dy].wait_recv()
            at = tile_of(h, t, ((z + 4 - dz) % 4) * 4 + (y + 4 - dy) % 4)
            ring[h, t, "sr", dz] = send(at, at, row_dev(0, dy))

    def s_end(h):
        for t in range(TILES):
            for dz in range(4):
                ring[h, t, "sy", dz, 3 if dz < 2 else 1].wait_recv()
                ring[h, t, "sr", dz].wait_recv()

    def product_back(h, t):
        lhs = s_all[h].reshape(-1, cols)
        q = lax.dot_general(lhs, basis[pl.ds(t * tw, tw), :], (((1,), (1,)), ((), ())), preferred_element_type=f32)
        back[h, t] = q.reshape(8, 2, hr, tw)
        ring[h, t, "c"] = send(back.at[h, t, :, (k + 1) % 2], crecv.at[h, t], col_dev(0, 0, 1))

    def core_end(h, t):
        ring[h, t, "c"].wait_recv()
        for far in range(2):
            for q in range(4):
                xsum[h, t, far, q] = back[h, t, far * 4 + q, k] + crecv[h, t, far * 4 + q]
        for dx in (1, 3, 2):
            for far in range(2):
                xsend[h, t, dx - 1, far] = xsum[h, t, far, (x + dx) % 4].astype(bf16)
            ring[h, t, "x", dx] = send(xsend.at[h, t, dx - 1], xrecv.at[h, t, dx - 1], col_dev(0, dx, 0))

    def x_end(h, t):
        for dx in (1, 3, 2):
            ring[h, t, "x", dx].wait_recv()
        for far in range(2):
            total = xsum[h, t, far, x]
            for dx in (1, 2, 3):
                total = total + xrecv[h, t, dx - 1, far].astype(f32)
            tsum[h, t, far] = total
        tsend[h, t] = tsum[h, t, (zh + 1) % 2].astype(bf16)
        ring[h, t, "t"] = send(tsend.at[h, t], trecv.at[h, t], col_dev(1, 0, 0))

    def finish(h, t):
        ring[h, t, "t"].wait_recv()
        total = tsum[h, t, zh] + trecv[h, t].astype(f32)
        out_ref[pl.ds(h * hr, hr), pl.ds(t * tw, tw)] = total.astype(bf16)

    spread_own(0)
    spread_far(0)
    spread_own(1)
    spread_near(0)
    spread_end(0)
    local[0].wait()
    product(0, 0)
    y_first(0, 0)
    spread_far(1)
    product(0, 1)
    y_first(0, 1)
    y_second(0, 0)
    spread_near(1)
    y_second(0, 1)
    spread_end(1)
    product(1, 0)
    y_first(1, 0)
    y_end(0, 0)
    product(1, 1)
    y_first(1, 1)
    local[1].wait()
    y_end(0, 1)
    y_second(1, 0)
    z_end(0, 0)
    y_second(1, 1)
    z_end(0, 1)
    z_spread(0, 0)
    y_end(1, 0)
    z_spread(0, 1)
    y_end(1, 1)
    y_relay(0, 0)
    z_end(1, 0)
    y_relay(0, 1)
    z_end(1, 1)
    z_spread(1, 0)
    z_spread(1, 1)
    s_end(0)
    product_back(0, 0)
    y_relay(1, 0)
    product_back(0, 1)
    y_relay(1, 1)
    core_end(0, 0)
    core_end(0, 1)
    x_end(0, 0)
    x_end(0, 1)
    s_end(1)
    product_back(1, 0)
    product_back(1, 1)
    core_end(1, 0)
    core_end(1, 1)
    finish(0, 0)
    finish(0, 1)
    x_end(1, 0)
    x_end(1, 1)
    finish(1, 0)
    finish(1, 1)
    for copy in started:
        copy.wait_send()


def per_device(gradient, basis, eigen):
    rows, cols = gradient.shape
    hr, tw = rows // HALVES, cols // TILES
    f32, bf16 = jnp.float32, jnp.bfloat16
    ht = (HALVES, TILES)
    any_space = pl.BlockSpec(memory_space=pl.ANY)
    return pl.pallas_call(
        kernel,
        out_shape=jax.ShapeDtypeStruct((rows, cols), bf16),
        in_specs=[any_space] * 3,
        out_specs=pl.BlockSpec(memory_space=pltpu.VMEM),
        scratch_shapes=[
            pltpu.VMEM(basis.shape, bf16),
            pltpu.VMEM(eigen.shape, f32),
            pltpu.VMEM((HALVES, 16, hr, cols), bf16),
            pltpu.VMEM((*ht, 4, 4, hr, tw), f32),
            pltpu.VMEM((*ht, 6, 2, hr, tw), bf16),
            pltpu.VMEM((*ht, 6, 2, hr, tw), bf16),
            pltpu.VMEM((*ht, 4, hr, tw), f32),
            pltpu.VMEM((*ht, 3, hr, tw), bf16),
            pltpu.VMEM((*ht, 3, hr, tw), bf16),
            pltpu.VMEM((HALVES, 16, hr, cols), bf16),
            pltpu.VMEM((*ht, 8, 2, hr, tw), f32),
            pltpu.VMEM((*ht, 8, hr, tw), f32),
            pltpu.VMEM((*ht, 2, 4, hr, tw), f32),
            pltpu.VMEM((*ht, 3, 2, hr, tw), bf16),
            pltpu.VMEM((*ht, 3, 2, hr, tw), bf16),
            pltpu.VMEM((*ht, hr, tw), bf16),
            pltpu.VMEM((*ht, hr, tw), bf16),
            pltpu.VMEM((*ht, 2, hr, tw), f32),
            pltpu.SemaphoreType.DMA((NSEM,)),
            pltpu.SemaphoreType.DMA((NSEM,)),
            pltpu.SemaphoreType.DMA((4,)),
        ],
        compiler_params=pltpu.CompilerParams(
            collective_id=0, has_side_effects=True, vmem_limit_bytes=60 << 20),
    )(gradient, basis, eigen)


def solution(mesh):
    return jax.shard_map(
        per_device,
        mesh=mesh,
        in_specs=(P("col", "row"), P("row", "col"), P("row", "col")),
        out_specs=P("col", "row"),
        check_vma=False,
    )
```

time: 265 us -> 85.6 us (0.32)
  blocking collectives: 151 us -> 0 us
  Pallas kernels: 0 us -> 82.4 us
  waiting for transfers between devices: 81.4 us -> 0 us
  between operations: 13.5 us -> 0.01 us
  matrix products: 11.6 us -> 0 us
  other arithmetic: 5.45 us -> 0 us
    all_to_all x5 -> x0, blocking collectives: 151 us -> none  [the longest x3 86.9 us: sent_to_all(): lax.all_to_all(jnp.broadcast_to(shard[None], (count, *shard.shape)), axis...]
    pallas_call x0 -> x1, Pallas kernels: none -> 82.4 us  [per_device(): pl.pallas_call(kernel, out_shape=jax.ShapeDtypeStruct((rows, cols), bf16)...]
    reduce_scatter x1 -> x0, waiting for transfers between devices: 81.4 us -> none  [per_device(): lax.psum_scatter(jnp.dot(part, basis, preferred_element_type=jnp.float32)...]
    dot_general x2 -> x0, matrix products: 11.6 us -> none  [the longest x1 6.34 us: per_device(): lax.dot_general(part, basis, (((1,), (1,)), ((), ())), preferred_element_...]
    reduce_sum x2 -> x0, other arithmetic: 4.47 us -> none  [the longest x1 3.72 us: sum_at_owner(): return arrived.sum(axis=0)]
  transfers between devices with their start and end apart: 1 -> 0, of which waited for: 1 -> 0; matrix products, arithmetic and copies ran while one was open for 0% -> 0% of each run, Pallas kernels for 0% -> 0%
where the time goes in v1:
time: 85.6 us; the launch traced here: 83.9 us
  Pallas kernels  82.4 us (96%)
  local copies, waits for them, and re-layouts  1.55 us (2%)
    pallas_call x1, Pallas kernels, per_device(): pl.pallas_call(kernel, out_shape=jax.ShapeDtypeStruct((rows, cols), bf16)...  82.4 us

profile of v1, /device:TPU:32, one launch (start us, length us, event | category | flops | bytes accessed | tf_op | source)
XLA Modules:
  0.0 83.9 jit_solution(7210627321057508455)
XLA Ops:
  0.0 82.4 %shard_map.37 = bf16[32,1792]{1,0:T(8,128)(2,1)} custom-call(bf16[32,1792]{1,0:T(8,128)(2,1)} %g_ref.1, bf16[1792,1792]{1,0:T(8,128)(2,1)} %b_ref.1, f32[32,1792]{1,0:T(8,128)} %e_ref.1), custom_call_target="tpu_custom_call" | custom-call | tf_op jit(solution)/shard_map/pallas_call | solution.py:269
  82.4 1.6 %copy.5 = bf16[32,1792]{1,0:T(8,128)(2,1)} copy(bf16[32,1792]{1,0:T(8,128)(2,1)} %shard_map.37) | data formatting | bytes 229376

commit v2 on v0

v2 whole, which is shorter than its diff:
```python
import functools

import jax
import jax.numpy as jnp
from jax import lax
from jax.experimental import pallas as pl
from jax.experimental.pallas import tpu as pltpu
from jax.sharding import PartitionSpec as P

MESH = pl.DeviceIdType.MESH
HALVES = 2
LANES = (7, 7)
TILES = len(LANES)
NSEM = 186


def kernel(g_ref, b_ref, e_ref, out_ref, basis, eigen, g_all, part, ysend, yrecv, ysum, zsend, zrecv, s_all,
           back, crecv, xsum, xsend, xrecv, tsend, trecv, ssem, rsem, lsem):
    f32, bf16 = jnp.float32, jnp.bfloat16
    cols = basis.shape[1]
    hr = g_all.shape[3]
    step = cols // sum(LANES)
    tiles = [pl.ds(sum(LANES[:t]) * step, LANES[t] * step) for t in range(TILES)]
    r, c = lax.axis_index("row"), lax.axis_index("col")
    z, y = r // 4, r % 4
    zh, x, k = c // 8, (c // 2) % 4, c % 2

    def row_dev(dz, dy):
        return (((z + dz) % 4) * 4 + (y + dy) % 4, c)

    def col_dev(dzh, dx, dk):
        return (r, ((zh + dzh) % 2) * 8 + ((x + dx) % 4) * 2 + (k + dk) % 2)

    started = []

    def send(src, dst, device):
        i = len(started)
        copy = pltpu.make_async_remote_copy(
            src_ref=src, dst_ref=dst, send_sem=ssem.at[i], recv_sem=rsem.at[i],
            device_id=device, device_id_type=MESH)
        copy.start()
        started.append(copy)
        return copy

    local = [pltpu.make_async_copy(g_ref.at[pl.ds(h * hr, hr)], g_all.at[h, zh, c % 8], lsem.at[2 + h]) for h in range(HALVES)]
    local += [pltpu.make_async_copy(e_ref, eigen, lsem.at[1]), pltpu.make_async_copy(b_ref, basis, lsem.at[0])]
    for copy in local:
        copy.start()

    barrier = pltpu.get_barrier_semaphore()
    peers = [row_dev(0, 1), row_dev(0, 3), row_dev(1, 0), row_dev(2, 0), row_dev(3, 0),
             col_dev(1, 0, 0), col_dev(0, 1, 0), col_dev(0, 2, 0), col_dev(0, 3, 0), col_dev(0, 0, 1)]
    for peer in peers:
        pl.semaphore_signal(barrier, inc=1, device_id=peer, device_id_type=MESH)
    pl.semaphore_wait(barrier, len(peers))

    ring = {}
    seen = set()

    def once(copy):
        if id(copy) not in seen:
            seen.add(id(copy))
            copy.wait()

    def own(h):
        mine, there = g_ref.at[pl.ds(h * hr, hr)], g_all.at[h, zh, c % 8]
        for dx in (1, 3, 2):
            ring["x", h, 0, dx] = send(mine, there, col_dev(0, dx, 0))
        ring["s", h, 0, 0] = send(mine, there, col_dev(0, 0, 1))
        ring["z", h] = send(mine, there, col_dev(1, 0, 0))

    def far(h):
        ring["z", h].wait_recv()
        at = g_all.at[h, (zh + 1) % 2, c % 8]
        for dx in (1, 3, 2):
            ring["x", h, 1, dx] = send(at, at, col_dev(0, dx, 0))
        ring["s", h, 1, 0] = send(at, at, col_dev(0, 0, 1))

    def near(h, u, dx):
        ring["x", h, u, dx].wait_recv()
        at = g_all.at[h, (zh + u) % 2, ((x + 4 - dx) % 4) * 2 + k]
        ring["s", h, u, dx] = send(at, at, col_dev(0, 0, 1))

    def product(h, u, t):
        if t == 0:
            for i in range(4):
                ring["s", h, u, i].wait_recv()
            if u == 0:
                once(local[h])
        once(local[HALVES + 1])
        lhs = g_all[h, (zh + u) % 2].reshape(-1, cols)
        p = jnp.dot(lhs, basis[:, tiles[t]], preferred_element_type=f32)
        part[h, u, t] = p.reshape(2, 4, hr, -1)
        up, down, across = (y + 1) % 4, (y + 3) % 4, (y + 2) % 4
        for i, (q, d, dy) in enumerate(((0, across, 1), (1, across, 3), (1, up, 1), (0, down, 3))):
            ysend[h, u, t, i] = part[h, u, t, q, d].astype(bf16)
            ring["r", h, u, t, i] = send(ysend.at[h, u, t, i], yrecv.at[h, u, t, i], row_dev(0, dy))

    def y_second(h, u, t, q):
        dy = 1 + 2 * q
        ring["r", h, u, t, q].wait_recv()
        ysend[h, u, t, 4 + q] = (
            part[h, u, t, q, (y + dy) % 4] + yrecv[h, u, t, q].astype(f32)).astype(bf16)
        ring["r", h, u, t, 4 + q] = send(
            ysend.at[h, u, t, 4 + q], yrecv.at[h, u, t, 4 + q], row_dev(0, dy))

    def y_end(h, u, t):
        for i in (2, 3, 4, 5):
            ring["r", h, u, t, i].wait_recv()
        for q in range(2):
            ysum[h, t, ((zh + u) % 2) * 2 + q] = (
                part[h, u, t, q, y] + yrecv[h, u, t, 3 - q].astype(f32)
                + yrecv[h, u, t, 4 + q].astype(f32))

    def z_first(h, t):
        for dz in (2, 1, 3):
            zsend[h, t, dz - 1] = ysum[h, t, (z + dz) % 4].astype(bf16)
            ring["zr", h, t, dz] = send(
                zsend.at[h, t, dz - 1], zrecv.at[h, t, dz - 1], row_dev(dz, 0))

    def tile_of(h, t, z1, y1):
        return s_all.at[h, z1 // 2, (z1 % 2) * 4 + y1, :, tiles[t]]

    def y_spread(h, t, dz):
        at = tile_of(h, t, (z + 4 - dz) % 4, y)
        for dy in (1, 3):
            ring["sy", h, t, dz, dy] = send(at, at, row_dev(0, dy))

    def z_end(h, t):
        once(local[HALVES])
        total = ysum[h, t, z]
        for dz in (1, 2, 3):
            ring["zr", h, t, dz].wait_recv()
            total = total + zrecv[h, t, dz - 1].astype(f32)
        scaled = total / eigen[pl.ds(h * hr, hr), tiles[t]]
        s_all[h, z // 2, (z % 2) * 4 + y, :, tiles[t]] = scaled.astype(bf16)
        at = tile_of(h, t, z, y)
        for dz in (2, 1, 3):
            ring["sz", h, t, dz] = send(at, at, row_dev(dz, 0))
        y_spread(h, t, 0)

    def z_spread(h, t, dz):
        ring["sz", h, t, dz].wait_recv()
        y_spread(h, t, dz)

    def y_relay(h, t, dz):
        dy = 1 if dz < 2 else 3
        ring["sy", h, t, dz, dy].wait_recv()
        at = tile_of(h, t, (z + 4 - dz) % 4, (y + 4 - dy) % 4)
        ring["sr", h, t, dz] = send(at, at, row_dev(0, dy))

    def s_end(h):
        if ("end", h) not in seen:
            seen.add(("end", h))
            for t in range(TILES):
                for dz in range(4):
                    ring["sy", h, t, dz, 3 if dz < 2 else 1].wait_recv()
                    ring["sr", h, t, dz].wait_recv()

    def product_back(h, u, t):
        s_end(h)
        lhs = s_all[h, (zh + u) % 2].reshape(-1, cols)
        q = lax.dot_general(lhs, basis[tiles[t], :], (((1,), (1,)), ((), ())), preferred_element_type=f32)
        back[h, u, t] = q.reshape(4, 2, hr, -1)
        ring["c", h, u, t] = send(
            back.at[h, u, t, :, (k + 1) % 2], crecv.at[h, u, t], col_dev(0, 0, 1))

    def core_end(h, u, t):
        ring["c", h, u, t].wait_recv()
        for dx in (1, 3, 2, 0):
            to = (x + dx) % 4
            total = back[h, u, t, to, k] + crecv[h, u, t, to]
            if dx == 0:
                xsum[h, u, t] = total
            else:
                xsend[h, u, t, dx - 1] = total.astype(bf16)
                ring["rx", h, u, t, dx] = send(
                    xsend.at[h, u, t, dx - 1], xrecv.at[h, u, t, dx - 1], col_dev(0, dx, 0))

    def x_end(h, u, t):
        total = xsum[h, u, t]
        for dx in (1, 3, 2):
            ring["rx", h, u, t, dx].wait_recv()
            total = total + xrecv[h, u, t, dx - 1].astype(f32)
        if u == 1:
            tsend[h, t] = total.astype(bf16)
            ring["t", h, t] = send(tsend.at[h, t], trecv.at[h, t], col_dev(1, 0, 0))
        else:
            ring["t", h, t].wait_recv()
            total = total + trecv[h, t].astype(f32)
            out_ref[pl.ds(h * hr, hr), tiles[t]] = total.astype(bf16)

    own(0)
    near(0, 0, 1)
    near(0, 0, 3)
    near(0, 0, 2)
    own(1)
    product(0, 0, 0)
    far(0)
    product(0, 0, 1)
    near(1, 0, 1)
    near(1, 0, 3)
    near(1, 0, 2)
    y_second(0, 0, 0, 0)
    y_second(0, 0, 0, 1)
    y_second(0, 0, 1, 0)
    y_second(0, 0, 1, 1)
    product(1, 0, 0)
    far(1)
    near(0, 1, 1)
    near(0, 1, 3)
    near(0, 1, 2)
    y_end(0, 0, 0)
    product(1, 0, 1)
    y_end(0, 0, 1)
    y_second(1, 0, 0, 0)
    product(0, 1, 0)
    y_second(1, 0, 0, 1)
    y_second(1, 0, 1, 0)
    y_second(1, 0, 1, 1)
    near(1, 1, 1)
    near(1, 1, 3)
    near(1, 1, 2)
    product(0, 1, 1)
    y_second(0, 1, 0, 0)
    y_second(0, 1, 0, 1)
    y_end(1, 0, 0)
    y_second(0, 1, 1, 0)
    y_second(0, 1, 1, 1)
    y_end(1, 0, 1)
    y_end(0, 1, 0)
    z_first(0, 0)
    product(1, 1, 0)
    y_end(0, 1, 1)
    z_first(0, 1)
    product(1, 1, 1)
    y_second(1, 1, 0, 0)
    y_second(1, 1, 0, 1)
    y_second(1, 1, 1, 0)
    y_second(1, 1, 1, 1)
    z_end(0, 0)
    z_end(0, 1)
    y_end(1, 1, 0)
    z_first(1, 0)
    z_spread(0, 0, 1)
    z_spread(0, 0, 3)
    z_spread(0, 0, 2)
    y_end(1, 1, 1)
    z_first(1, 1)
    z_spread(0, 1, 1)
    z_spread(0, 1, 3)
    z_spread(0, 1, 2)
    y_relay(0, 0, 0)
    y_relay(0, 0, 1)
    y_relay(0, 0, 3)
    y_relay(0, 0, 2)
    y_relay(0, 1, 0)
    z_end(1, 0)
    y_relay(0, 1, 1)
    y_relay(0, 1, 3)
    y_relay(0, 1, 2)
    z_end(1, 1)
    z_spread(1, 0, 1)
    z_spread(1, 0, 3)
    z_spread(1, 0, 2)
    z_spread(1, 1, 1)
    z_spread(1, 1, 3)
    z_spread(1, 1, 2)
    product_back(0, 1, 0)
    y_relay(1, 0, 0)
    y_relay(1, 0, 1)
    y_relay(1, 0, 3)
    y_relay(1, 0, 2)
    product_back(0, 1, 1)
    y_relay(1, 1, 0)
    y_relay(1, 1, 1)
    y_relay(1, 1, 3)
    y_relay(1, 1, 2)
    product_back(0, 0, 0)
    core_end(0, 1, 0)
    product_back(0, 0, 1)
    core_end(0, 1, 1)
    core_end(0, 0, 0)
    product_back(1, 1, 0)
    product_back(1, 1, 1)
    core_end(1, 1, 0)
    product_back(1, 0, 0)
    core_end(1, 1, 1)
    product_back(1, 0, 1)
    core_end(0, 0, 1)
    x_end(0, 1, 0)
    x_end(0, 1, 1)
    core_end(1, 0, 0)
    core_end(1, 0, 1)
    x_end(1, 1, 0)
    x_end(1, 1, 1)
    x_end(0, 0, 0)
    x_end(0, 0, 1)
    x_end(1, 0, 0)
    x_end(1, 0, 1)
    for copy in started:
        copy.wait_send()


def per_device(gradient, basis, eigen):
    rows, cols = gradient.shape
    hr, tw = rows // HALVES, cols // TILES
    ht, hut = (HALVES, TILES), (HALVES, 2, TILES)
    f32, bf16 = jnp.float32, jnp.bfloat16
    any_space = pl.BlockSpec(memory_space=pl.ANY)
    return pl.pallas_call(
        kernel,
        out_shape=jax.ShapeDtypeStruct((rows, cols), bf16),
        in_specs=[any_space] * 3,
        out_specs=pl.BlockSpec(memory_space=pltpu.VMEM),
        scratch_shapes=[
            pltpu.VMEM(basis.shape, bf16),
            pltpu.VMEM(eigen.shape, f32),
            pltpu.VMEM((HALVES, 2, 8, hr, cols), bf16),
            pltpu.VMEM((*hut, 2, 4, hr, tw), f32),
            pltpu.VMEM((*hut, 6, hr, tw), bf16),
            pltpu.VMEM((*hut, 6, hr, tw), bf16),
            pltpu.VMEM((*ht, 4, hr, tw), f32),
            pltpu.VMEM((*ht, 3, hr, tw), bf16),
            pltpu.VMEM((*ht, 3, hr, tw), bf16),
            pltpu.VMEM((HALVES, 2, 8, hr, cols), bf16),
            pltpu.VMEM((*hut, 4, 2, hr, tw), f32),
            pltpu.VMEM((*hut, 4, hr, tw), f32),
            pltpu.VMEM((*hut, hr, tw), f32),
            pltpu.VMEM((*hut, 3, hr, tw), bf16),
            pltpu.VMEM((*hut, 3, hr, tw), bf16),
            pltpu.VMEM((*ht, hr, tw), bf16),
            pltpu.VMEM((*ht, hr, tw), bf16),
            pltpu.SemaphoreType.DMA((NSEM,)),
            pltpu.SemaphoreType.DMA((NSEM,)),
            pltpu.SemaphoreType.DMA((2 + HALVES,)),
        ],
        compiler_params=pltpu.CompilerParams(
            collective_id=0, has_side_effects=True, vmem_limit_bytes=60 << 20),
    )(gradient, basis, eigen)


def solution(mesh):
    return jax.shard_map(
        per_device,
        mesh=mesh,
        in_specs=(P("col", "row"), P("row", "col"), P("row", "col")),
        out_specs=P("col", "row"),
        check_vma=False,
    )
```

time: 265 us -> 80.7 us (0.30)
  blocking collectives: 151 us -> 0 us
  waiting for transfers between devices: 81.4 us -> 0 us
  Pallas kernels: 0 us -> 78.6 us
  between operations: 13.5 us -> 0.01 us
  matrix products: 11.6 us -> 0 us
  other arithmetic: 5.45 us -> 0 us
    all_to_all x5 -> x0, blocking collectives: 151 us -> none  [the longest x3 86.9 us: sent_to_all(): lax.all_to_all(jnp.broadcast_to(shard[None], (count, *shard.shape)), axis...]
    reduce_scatter x1 -> x0, waiting for transfers between devices: 81.4 us -> none  [per_device(): lax.psum_scatter(jnp.dot(part, basis, preferred_element_type=jnp.float32)...]
    pallas_call x0 -> x1, Pallas kernels: none -> 78.6 us  [per_device(): pl.pallas_call(kernel, out_shape=jax.ShapeDtypeStruct((rows, cols), bf16)...]
    dot_general x2 -> x0, matrix products: 11.6 us -> none  [the longest x1 6.34 us: per_device(): lax.dot_general(part, basis, (((1,), (1,)), ((), ())), preferred_element_...]
    reduce_sum x2 -> x0, other arithmetic: 4.47 us -> none  [the longest x1 3.72 us: sum_at_owner(): return arrived.sum(axis=0)]
  transfers between devices with their start and end apart: 1 -> 0, of which waited for: 1 -> 0; matrix products, arithmetic and copies ran while one was open for 0% -> 0% of each run, Pallas kernels for 0% -> 0%
where the time goes in v2:
time: 80.7 us; the launch traced here: 80.2 us
  Pallas kernels  78.6 us (97%)
  local copies, waits for them, and re-layouts  1.55 us (2%)
    pallas_call x1, Pallas kernels, per_device(): pl.pallas_call(kernel, out_shape=jax.ShapeDtypeStruct((rows, cols), bf16)...  78.6 us

profile of v2, /device:TPU:32, one launch (start us, length us, event | category | flops | bytes accessed | tf_op | source)
XLA Modules:
  0.0 80.2 jit_solution(917119195803616922)
XLA Ops:
  0.0 78.6 %shard_map.37 = bf16[32,1792]{1,0:T(8,128)(2,1)} custom-call(bf16[32,1792]{1,0:T(8,128)(2,1)} %g_ref.1, bf16[1792,1792]{1,0:T(8,128)(2,1)} %b_ref.1, f32[32,1792]{1,0:T(8,128)} %e_ref.1), custom_call_target="tpu_custom_call" | custom-call | tf_op jit(solution)/shard_map/pallas_call | solution.py:311
  78.6 1.6 %copy.5 = bf16[32,1792]{1,0:T(8,128)(2,1)} copy(bf16[32,1792]{1,0:T(8,128)(2,1)} %shard_map.37) | data formatting | bytes 229376

commit v3 on v2

--- a/solution.py
+++ b/solution.py
@@ -191,37 +191,37 @@
             out_ref[pl.ds(h * hr, hr), tiles[t]] = total.astype(bf16)
 
     own(0)
+    own(1)
     near(0, 0, 1)
     near(0, 0, 3)
     near(0, 0, 2)
-    own(1)
+    far(0)
     product(0, 0, 0)
-    far(0)
+    near(1, 0, 3)
+    near(1, 0, 1)
     product(0, 0, 1)
-    near(1, 0, 1)
-    near(1, 0, 3)
     near(1, 0, 2)
+    product(1, 0, 0)
     y_second(0, 0, 0, 0)
+    near(0, 1, 1)
+    near(0, 1, 3)
     y_second(0, 0, 0, 1)
+    far(1)
     y_second(0, 0, 1, 0)
     y_second(0, 0, 1, 1)
-    product(1, 0, 0)
-    far(1)
-    near(0, 1, 1)
-    near(0, 1, 3)
     near(0, 1, 2)
+    product(1, 0, 1)
+    product(0, 1, 0)
     y_end(0, 0, 0)
-    product(1, 0, 1)
+    y_second(1, 0, 0, 0)
+    y_second(1, 0, 0, 1)
+    product(0, 1, 1)
     y_end(0, 0, 1)
-    y_second(1, 0, 0, 0)
-    product(0, 1, 0)
-    y_second(1, 0, 0, 1)
     y_second(1, 0, 1, 0)
     y_second(1, 0, 1, 1)
     near(1, 1, 1)
     near(1, 1, 3)
     near(1, 1, 2)
-    product(0, 1, 1)
     y_second(0, 1, 0, 0)
     y_second(0, 1, 0, 1)
     y_end(1, 0, 0)
@@ -242,11 +242,11 @@
     z_end(0, 1)
     y_end(1, 1, 0)
     z_first(1, 0)
+    y_end(1, 1, 1)
+    z_first(1, 1)
     z_spread(0, 0, 1)
     z_spread(0, 0, 3)
     z_spread(0, 0, 2)
-    y_end(1, 1, 1)
-    z_first(1, 1)
     z_spread(0, 1, 1)
     z_spread(0, 1, 3)
     z_spread(0, 1, 2)

time: 80.7 us -> 79.8 us (0.989)
  no operation moved by 1% of the time
where the time goes in v3:
time: 79.8 us; the launch traced here: 79.5 us
  Pallas kernels  77.9 us (98%)
  local copies, waits for them, and re-layouts  1.55 us (2%)
    pallas_call x1, Pallas kernels, per_device(): pl.pallas_call(kernel, out_shape=jax.ShapeDtypeStruct((rows, cols), bf16)...  77.9 us

profile of v3, /device:TPU:32, one launch (start us, length us, event | category | flops | bytes accessed | tf_op | source)
XLA Modules:
  0.0 79.5 jit_solution(16609664296014889500)
XLA Ops:
  0.0 77.9 %shard_map.37 = bf16[32,1792]{1,0:T(8,128)(2,1)} custom-call(bf16[32,1792]{1,0:T(8,128)(2,1)} %g_ref.1, bf16[1792,1792]{1,0:T(8,128)(2,1)} %b_ref.1, f32[32,1792]{1,0:T(8,128)} %e_ref.1), custom_call_target="tpu_custom_call" | custom-call | tf_op jit(solution)/shard_map/pallas_call | solution.py:311
  78.0 1.6 %copy.5 = bf16[32,1792]{1,0:T(8,128)(2,1)} copy(bf16[32,1792]{1,0:T(8,128)(2,1)} %shard_map.37) | data formatting | bytes 229376

commit v4 on v3

--- a/solution.py
+++ b/solution.py
@@ -64,7 +64,7 @@
 
     def own(h):
         mine, there = g_ref.at[pl.ds(h * hr, hr)], g_all.at[h, zh, c % 8]
-        for dx in (1, 3, 2):
+        for dx in (2, 1, 3):
             ring["x", h, 0, dx] = send(mine, there, col_dev(0, dx, 0))
         ring["s", h, 0, 0] = send(mine, there, col_dev(0, 0, 1))
         ring["z", h] = send(mine, there, col_dev(1, 0, 0))
@@ -72,7 +72,7 @@
     def far(h):
         ring["z", h].wait_recv()
         at = g_all.at[h, (zh + 1) % 2, c % 8]
-        for dx in (1, 3, 2):
+        for dx in (2, 1, 3):
             ring["x", h, 1, dx] = send(at, at, col_dev(0, dx, 0))
         ring["s", h, 1, 0] = send(at, at, col_dev(0, 0, 1))
 
@@ -167,7 +167,7 @@
 
     def core_end(h, u, t):
         ring["c", h, u, t].wait_recv()
-        for dx in (1, 3, 2, 0):
+        for dx in (2, 1, 3, 0):
             to = (x + dx) % 4
             total = back[h, u, t, to, k] + crecv[h, u, t, to]
             if dx == 0:
@@ -179,7 +179,7 @@
 
     def x_end(h, u, t):
         total = xsum[h, u, t]
-        for dx in (1, 3, 2):
+        for dx in (2, 1, 3):
             ring["rx", h, u, t, dx].wait_recv()
             total = total + xrecv[h, u, t, dx - 1].astype(f32)
         if u == 1:
@@ -192,24 +192,24 @@
 
     own(0)
     own(1)
+    near(0, 0, 2)
     near(0, 0, 1)
     near(0, 0, 3)
-    near(0, 0, 2)
     far(0)
     product(0, 0, 0)
+    near(1, 0, 1)
+    near(1, 0, 2)
+    product(0, 0, 1)
     near(1, 0, 3)
-    near(1, 0, 1)
-    product(0, 0, 1)
-    near(1, 0, 2)
     product(1, 0, 0)
     y_second(0, 0, 0, 0)
+    near(0, 1, 2)
     near(0, 1, 1)
-    near(0, 1, 3)
     y_second(0, 0, 0, 1)
     far(1)
     y_second(0, 0, 1, 0)
     y_second(0, 0, 1, 1)
-    near(0, 1, 2)
+    near(0, 1, 3)
     product(1, 0, 1)
     product(0, 1, 0)
     y_end(0, 0, 0)
@@ -219,9 +219,9 @@
     y_end(0, 0, 1)
     y_second(1, 0, 1, 0)
     y_second(1, 0, 1, 1)
+    near(1, 1, 2)
     near(1, 1, 1)
     near(1, 1, 3)
-    near(1, 1, 2)
     y_second(0, 1, 0, 0)
     y_second(0, 1, 0, 1)
     y_end(1, 0, 0)

time: 79.8 us -> 79.4 us (level)
  no operation moved by 1% of the time
where the time goes in v4:
time: 79.4 us; the launch traced here: 79.2 us
  Pallas kernels  77.6 us (98%)
  local copies, waits for them, and re-layouts  1.55 us (2%)
    pallas_call x1, Pallas kernels, per_device(): pl.pallas_call(kernel, out_shape=jax.ShapeDtypeStruct((rows, cols), bf16)...  77.6 us

profile of v4, /device:TPU:32, one launch (start us, length us, event | category | flops | bytes accessed | tf_op | source)
XLA Modules:
  0.0 79.2 jit_solution(15224863474614421597)
XLA Ops:
  0.0 77.6 %shard_map.37 = bf16[32,1792]{1,0:T(8,128)(2,1)} custom-call(bf16[32,1792]{1,0:T(8,128)(2,1)} %g_ref.1, bf16[1792,1792]{1,0:T(8,128)(2,1)} %b_ref.1, f32[32,1792]{1,0:T(8,128)} %e_ref.1), custom_call_target="tpu_custom_call" | custom-call | tf_op jit(solution)/shard_map/pallas_call | solution.py:311
  77.6 1.6 %copy.5 = bf16[32,1792]{1,0:T(8,128)(2,1)} copy(bf16[32,1792]{1,0:T(8,128)(2,1)} %shard_map.37) | data formatting | bytes 229376
